TPU v7x, 256 devices: a whole 4x4x8 slice. The times are simulated.
256 devices in a mesh: freq: 64 (over x, z, y_lo), panel: 4 (over y_hi, core).
Axes of the slice: x: 4, y: 4 (y_hi: 2, y_lo: 2; y = y_hi * 2 + y_lo), z: 8, core: 2. Of those that a mesh axis runs over, the one named last changes fastest.
Arguments:
- reflection: bfloat16 [2, 64, 1024, 1024], P(None, 'freq', None, 'panel'), may hold values from -0.1875 to 0.1875
- tile_mask: int32 [64, 16, 16], P('freq', None, 'panel'), may hold values 0 or 1
- focusing: bfloat16 [2, 64, 1024, 256], P(None, 'freq', 'panel'), may hold values from -6 to 6
- initial: float32 [2, 64, 1024, 256], P(None, 'freq', 'panel'), may hold values from -6 to 6
- onsets: int32 [1024, 256], P(('freq', 'panel')), may hold values from 1 to 64
Outputs:
- updated: float32 [2, 64, 1024, 256], P(None, 'freq', 'panel')
All inputs are finite; a program needn't handle non-finite values. No bound on the sum of `tile_mask` on one device may be relied on, other than what follows from the above.
Results may differ from a plain program's by a relative error of at most 0.0015.
Values may be sent and summed in bfloat16 or wider, within the bound.
No kernel may reach another device: no remote copies, remote signals or barrier semaphores. Data moves between devices by JAX's collectives and lax.ppermute only.
A program may use at most 64 MiB of HBM per device.

v0:
```python
import math

import jax
import jax.numpy as jnp
from jax import lax
from jax.sharding import PartitionSpec as P


def tables(length):
    counter = lax.iota(jnp.int32, length)
    product_mod = counter[:, None] * counter[None, :] % length
    angles = product_mod.astype(jnp.float32) * (2.0 * math.pi / length)
    return (jnp.cos(angles), jnp.sin(angles))


def exact_dot(operator_matrix, multiplied_input):
    return jnp.dot(
        operator_matrix,
        multiplied_input,
        precision=lax.Precision.HIGHEST,
        preferred_element_type=jnp.float32,
    )


def window_traces(traces, trace_onsets):
    length = traces.shape[1]
    trace_rows = traces.shape[3] * traces.shape[4]
    flat_rows = traces.reshape(2, length, trace_rows)
    cosine, sine = tables(length)
    real_t = (exact_dot(cosine, flat_rows[0]) - exact_dot(sine, flat_rows[1])) / length
    imaginary_trace_part = (
        exact_dot(sine, flat_rows[0]) + exact_dot(cosine, flat_rows[1])
    ) / length
    window = lax.iota(jnp.int32, length)[:, None] < trace_onsets.reshape(1, trace_rows)
    real_t = jnp.where(window, real_t, 0.0)
    imaginary_trace_part = jnp.where(window, imaginary_trace_part, 0.0)
    out_real = exact_dot(cosine, real_t) + exact_dot(sine, imaginary_trace_part)
    out_imag = exact_dot(cosine, imaginary_trace_part) - exact_dot(sine, real_t)
    return jnp.stack([out_real, out_imag]).astype(jnp.bfloat16).reshape(traces.shape)


def product(operator_matrix, multiplied_input):
    return jnp.einsum(
        "bqx,bxj->bqj", operator_matrix, multiplied_input, preferred_element_type=jnp.float32
    )


def contract(operator_matrix, multiplied_input):
    return jnp.einsum(
        "fabr,fabv->frv", operator_matrix, multiplied_input, preferred_element_type=jnp.float32
    )


def local(reflection, tile_mask, focusing, initial, onsets):
    per_device = reflection.shape[1]
    sources = reflection.shape[2]
    columns = reflection.shape[3]
    tile_edge_length = sources // tile_mask.shape[1]
    points = focusing.shape[3]
    filled = jnp.broadcast_to(
        tile_mask.astype(jnp.bfloat16)[:, :, None, :, None],
        (per_device, tile_mask.shape[1], tile_edge_length, tile_mask.shape[2], tile_edge_length),
    ).reshape(per_device, sources, columns)
    real_r = reflection[0] * filled
    imag_r = reflection[1] * filled
    real_g = product(real_r, focusing[0]) - product(imag_r, focusing[1])
    imag_g = product(real_r, focusing[1]) + product(imag_r, focusing[0])
    groups = lax.axis_size("freq")
    group_rows = sources // groups
    partial_g = jnp.stack([real_g, imag_g]).reshape(2, per_device, groups, group_rows, points)
    summed = lax.psum(partial_g, "panel")
    trace_onsets = lax.all_gather(onsets, "panel", axis=0, tiled=True)
    traces = lax.all_to_all(summed, "freq", split_axis=2, concat_axis=1, tiled=True)
    windowed = window_traces(traces, trace_onsets)
    returned_output = lax.all_to_all(windowed, "freq", split_axis=1, concat_axis=2, tiled=True)
    rows_real = real_r.reshape(per_device, groups, group_rows, columns)
    rows_imag = imag_r.reshape(per_device, groups, group_rows, columns)
    out_real = contract(rows_real, returned_output[0]) + contract(rows_imag, returned_output[1])
    out_imag = contract(rows_real, returned_output[1]) - contract(rows_imag, returned_output[0])
    return initial + jnp.stack([out_real, out_imag])


def solution(mesh):
    return jax.shard_map(
        local,
        mesh=mesh,
        in_specs=(
            P(None, "freq", None, "panel"),
            P("freq", None, "panel"),
            P(None, "freq", "panel", None),
            P(None, "freq", "panel", None),
            P(("freq", "panel"), None),
        ),
        out_specs=P(None, "freq", "panel", None),
        check_vma=False,
    )
```

profile of v0, /device:TPU:1, one launch (start us, length us, event | category | flops | bytes accessed | tf_op | source)
XLA Modules:
  0.0 194.5 jit_solution(1034007891396239297)
XLA Ops:
  6.5 0.8 convert_bitcast_fusion
  7.4 0.3 broadcast_in_dim.19
  7.8 0.7 broadcast_in_dim.20
  9.9 1.5 pad_maximum_fusion
  11.4 68.2 %all-reduce.2.cloned.1.call-done = f32[2,1,64,16,256]{4,3,1,0,2:T(8,128)} async-done(((f32[2,1,64,16,256]{4,3,1,0,2:T(8,128)}), f32[2,1,64,16,256]{4,3,1,0,2:T(8,128)}) %all-reduce.2.cloned.1.call-update) | async-done | bytes 2097168 | tf_op jit(solution)/shard_map/psum | solution.py:71
  79.6 10.2 %all-to-all-start = ((f32[2,1,64,16,256]{4,3,1,0,2:T(8,128)}), f32[2,1,64,16,256]{4,3,1,0,2:T(8,128)S(1)}, u32[]{:S(2)}, u32[]{:S(2)}) async-start(f32[2,1,64,16,256]{4,3,1,0,2:T(8,128)} %all-reduce.2.cloned.1.call-done), calls=%async_computation | async-start | bytes 4194304 | tf_op jit(solution)/shard_map/all_to_all | solution.py:73
  89.8 7.6 %all-gather = s32[4,4,256]{2,1,0:T(4,128)S(1)} all-gather(s32[1,4,256]{2,1,0:T(4,128)S(1)} %bitcast.114), channel_id=1, replica_groups=mesh['freq'=64,'panel'=4] {'panel'}, dimensions={0}, use_global_device_ids=true | all-gather | bytes 20480 | tf_op jit(solution)/shard_map/all_gather | solution.py:72
  97.4 42.3 %all-to-all-done = f32[2,1,64,16,256]{4,3,1,0,2:T(8,128)S(1)} async-done(((f32[2,1,64,16,256]{4,3,1,0,2:T(8,128)}), f32[2,1,64,16,256]{4,3,1,0,2:T(8,128)S(1)}, u32[]{:S(2)}, u32[]{:S(2)}) %all-to-all-start) | async-done | bytes 2097184 | tf_op jit(solution)/shard_map/all_to_all | solution.py:73
  139.9 0.6 copy.35
  140.5 1.1 fusion.41
  141.6 1.2 fusion.37
  142.8 0.6 copy.36
  143.4 1.3 fusion.3
  144.7 1.2 fusion.2
  145.9 1.2 fusion.35
  147.1 1.2 fusion.32
  148.3 1.2 fusion.4
  149.5 1.1 fusion.5
  150.9 33.7 %all_to_all.8 = bf16[2,64,1,16,256]{4,3,2,0,1:T(8,128)(2,1)S(1)} all-to-all(bf16[2,64,1,16,256]{4,3,2,0,1:T(8,128)(2,1)S(1)} %pad_maximum_fusion.1), channel_id=1, replica_groups=mesh['freq'=64,'panel'=4] {'freq'}, dimensions={1} | all-to-all | bytes 2097152 | tf_op jit(solution)/shard_map/all_to_all | solution.py:75
  185.0 0.3 convolution_bitcast_fusion
  185.4 0.3 fusion.9
  185.7 0.3 fusion.7
  186.1 0.7 copy-done.2
  186.8 0.9 maximum_add_fusion
  (21 shorter events, 2.4 us)
Async XLA Ops:
  6.5 1.9 copy-start
  6.5 73.1 %all-reduce.2.cloned.1.call-start = ((), (), s32[]{:S(2)}) async-start(), calls=%async_computation.2 | async-start | bytes 4194304 | tf_op jit(solution)/shard_map/psum | solution.py:71
  7.8 1.0 copy-start.1
  11.4 78.4 %copy-start.3 = (s32[4,256]{1,0:T(4,128)S(1)}, s32[4,256]{1,0:T(4,128)}, u32[]{:S(2)}) copy-start(s32[4,256]{1,0:T(4,128)} %param.9) | copy-start | bytes 12292
  79.6 60.1 %all-to-all-start = ((f32[2,1,64,16,256]{4,3,1,0,2:T(8,128)}), f32[2,1,64,16,256]{4,3,1,0,2:T(8,128)S(1)}, u32[]{:S(2)}, u32[]{:S(2)}) async-start(f32[2,1,64,16,256]{4,3,1,0,2:T(8,128)} %all-reduce.2.cloned.1.call-done), calls=%async_computation | async-start | bytes 4194304 | tf_op jit(solution)/shard_map/all_to_all | solution.py:73
  185.7 1.0 copy-start.2
Sparse Core Ops, SparseCore 0:
  11.5 68.0 all-reduce.1
where the time goes:
time: 195 us; the launch traced here: 194 us
  waiting for transfers between devices  110 us (56%)
  blocking collectives  41.3 us (21%)
  between operations  13.6 us (7%)
  matrix products  12 us (6%)
  starting transfers between devices  10.2 us (5%)
  local copies, waits for them, and re-layouts  3.57 us (2%)
  other arithmetic  3.3 us (2%)
    psum x1, waiting for transfers between devices, local(): summed = lax.psum(partial_g, 'panel')  68.2 us
    all_to_all x1, waiting for transfers between devices, local(): lax.all_to_all(summed, 'freq', split_axis=2, concat_axis=1, tiled=True)  42.3 us
    all_to_all x1, blocking collectives, local(): lax.all_to_all(windowed, 'freq', split_axis=1, concat_axis=2, tiled=True)  33.7 us
    all_to_all x1, starting transfers between devices, local(): lax.all_to_all(summed, 'freq', split_axis=2, concat_axis=1, tiled=True)  10.2 us
    dot_general x8, matrix products, exact_dot(): jnp.dot(operator_matrix, multiplied_input, precision=lax.Precision.HIGHES...  9.47 us
    all_gather x1, blocking collectives, local(): trace_onsets = lax.all_gather(onsets, 'panel', axis=0, tiled=True)  7.56 us
  transfers between devices with their start and end apart: 2, of which 2 were waited for; matrix products, arithmetic and copies ran while one was open for 0% of the time, Pallas kernels for 0%

commit v1 on v0

v1 whole, which is shorter than its diff:
```python
import math

import jax
import jax.numpy as jnp
import numpy as np
from jax import lax
from jax.sharding import PartitionSpec as P

SCALE = 16.0
CORE = ((0, 1), (1, 0), (2, 3), (3, 2))
CHIP = ((0, 2), (1, 3), (2, 0), (3, 1))


def transform(length, rows, sign):
    counter = np.arange(length)
    angles = (counter[:, None] * counter[None, :] % length) * (2.0 * math.pi / length)
    cosine, sine = np.cos(angles), sign * np.sin(angles)
    small = np.stack([np.stack([cosine, -sine], -1), np.stack([sine, cosine], -1)], 1)
    full = np.einsum("acbd,jk->acjbdk", small, np.eye(rows))
    return full.reshape(2 * length * rows, 2 * length * rows).astype(np.float32)


def exact_dot(left, right):
    return jnp.dot(left, right, precision=lax.Precision.HIGHEST, preferred_element_type=jnp.float32)


def local(reflection, tile_mask, focusing, initial, onsets):
    sources, columns = reflection.shape[2], reflection.shape[3]
    points = focusing.shape[3]
    edge = sources // tile_mask.shape[1]
    groups = lax.axis_size("freq")
    panels = lax.axis_size("panel")
    rows = sources // groups // panels
    panel = lax.axis_index("panel")

    filled = jnp.broadcast_to(
        tile_mask[0].astype(jnp.bfloat16)[:, None, :, None],
        (tile_mask.shape[1], edge, tile_mask.shape[2], edge),
    ).reshape(sources, columns)
    masked = reflection[:, 0] * filled
    masked = masked.reshape(2, groups, 2, 2, rows, columns)
    masked = jnp.where(panel // 2 == 0, masked, masked[:, :, ::-1])
    masked = jnp.where(panel % 2 == 0, masked, masked[:, :, :, ::-1])
    masked = masked.transpose(2, 3, 1, 0, 4, 5)
    turned = jnp.stack([-masked[:, :, :, 1], masked[:, :, :, 0]], 3)
    block = groups * 2 * rows
    operator = jnp.concatenate([masked, turned], -1).reshape(2, 2, block, 2 * columns)

    fields = focusing.reshape(2 * columns, points)
    partial = jnp.einsum("hcsr,rv->hcsv", operator, fields, preferred_element_type=jnp.float32)
    partial = partial * SCALE
    other = lax.ppermute(partial[:, 1].astype(jnp.float16), "panel", CORE)
    partial = partial[:, 0] + other.astype(jnp.float32)
    other = lax.ppermute(partial[1].astype(jnp.float16), "panel", CHIP)
    partial = partial[0] + other.astype(jnp.float32)

    traces = lax.all_to_all(
        partial.astype(jnp.float16).reshape(groups, 2 * rows, points), "freq",
        split_axis=0, concat_axis=0, tiled=True,
    ).reshape(block, points)
    to_time = jnp.asarray(transform(groups, rows, 1) / (SCALE * groups))
    to_freq = jnp.asarray(transform(groups, rows, -1))
    series = exact_dot(to_time, traces.astype(jnp.float32)).reshape(groups, 2, rows, points)
    inside = lax.broadcasted_iota(jnp.int32, series.shape, 0) < onsets
    series = jnp.where(inside, series, 0.0).reshape(block, points)
    windowed = exact_dot(to_freq, series).astype(jnp.bfloat16)

    own = lax.all_to_all(
        windowed.reshape(groups, 2 * rows, points), "freq", split_axis=0, concat_axis=0, tiled=True
    ).reshape(block, points)
    pair = jnp.stack([own, lax.ppermute(own, "panel", CHIP)])
    every = jnp.stack([pair, lax.ppermute(pair, "panel", CORE)], 1)
    adjoint = jnp.einsum("hcsr,hcsv->rv", operator, every, preferred_element_type=jnp.float32)
    return initial + adjoint.reshape(initial.shape)


def solution(mesh):
    return jax.shard_map(
        local,
        mesh=mesh,
        in_specs=(
            P(None, "freq", None, "panel"),
            P("freq", None, "panel"),
            P(None, "freq", "panel", None),
            P(None, "freq", "panel", None),
            P(("freq", "panel"), None),
        ),
        out_specs=P(None, "freq", "panel", None),
        check_vma=False,
    )
```

time: 195 us -> 83.5 us (0.43)
  waiting for transfers between devices: 110 us -> 22.8 us
  blocking collectives: 41.3 us -> 17.2 us
  between operations: 13.6 us -> 0.2 us
  starting transfers between devices: 10.2 us -> 23.2 us
  matrix products: 12 us -> 8.2 us
  local copies, waits for them, and re-layouts: 3.57 us -> 6.82 us
    psum x1 -> x0, waiting for transfers between devices: 68.2 us -> none  [local(): summed = lax.psum(partial_g, 'panel')]
    all_to_all x1, waiting for transfers between devices: 42.3 us -> 9.32 us  [local(): lax.all_to_all(partial.astype(jnp.float16).reshape(groups, 2 * rows, poin...]
    all_to_all x1, blocking collectives: 33.7 us -> 17.2 us  [local(): lax.all_to_all(windowed.reshape(groups, 2 * rows, points), 'freq', split_...]
    ppermute x0 -> x4, waiting for transfers between devices: none -> 13.5 us  [the longest x1 7.79 us: local(): other = lax.ppermute(partial[1].astype(jnp.float16), 'panel', CHIP)]
    ppermute x0 -> x4, starting transfers between devices: none -> 12 us  [the longest x1 4.79 us: local(): every = jnp.stack([pair, lax.ppermute(pair, 'panel', CORE)], 1)]
    all_gather x1 -> x0, blocking collectives: 7.56 us -> none  [local(): trace_onsets = lax.all_gather(onsets, 'panel', axis=0, tiled=True)]
    dot_general x16 -> x4, matrix products: 12 us -> 8.2 us  [the longest x2 4.12 us: exact_dot(): jnp.dot(left, right, precision=lax.Precision.HIGHEST, preferred_element_t...]
    reshape x0 -> x1, local copies, waits for them, and re-layouts: none -> 2.54 us  [local(): jnp.concatenate([masked, turned], -1).reshape(2, 2, block, 2 * columns)]
  transfers between devices with their start and end apart: 2 -> 5, of which waited for: 2 -> 4; matrix products, arithmetic and copies ran while one was open for 0% -> 3% of each run, Pallas kernels for 0% -> 0%
where the time goes in v1:
time: 83.5 us; the launch traced here: 83.3 us
  starting transfers between devices  23.2 us (28%)
  waiting for transfers between devices  22.8 us (27%)
  blocking collectives  17.2 us (21%)
  matrix products  8.2 us (10%)
  local copies, waits for them, and re-layouts  6.82 us (8%)
  other arithmetic  4.82 us (6%)
    all_to_all x1, blocking collectives, local(): lax.all_to_all(windowed.reshape(groups, 2 * rows, points), 'freq', split_...  17.2 us
    all_to_all x1, starting transfers between devices, local(): lax.all_to_all(partial.astype(jnp.float16).reshape(groups, 2 * rows, poin...  11.2 us
    all_to_all x1, waiting for transfers between devices, local(): lax.all_to_all(partial.astype(jnp.float16).reshape(groups, 2 * rows, poin...  9.32 us
    ppermute x1, waiting for transfers between devices, local(): other = lax.ppermute(partial[1].astype(jnp.float16), 'panel', CHIP)  7.79 us
    ppermute x1, starting transfers between devices, local(): every = jnp.stack([pair, lax.ppermute(pair, 'panel', CORE)], 1)  4.79 us
    ppermute x1, waiting for transfers between devices, local(): pair = jnp.stack([own, lax.ppermute(own, 'panel', CHIP)])  4.15 us
    dot_general x2, matrix products, exact_dot(): jnp.dot(left, right, precision=lax.Precision.HIGHEST, preferred_element_t...  4.12 us
    dot_general x1, matrix products, local(): jnp.einsum('hcsr,hcsv->rv', operator, every, preferred_element_type=jnp.f...  3.37 us
  transfers between devices with their start and end apart: 5, of which 4 were waited for; matrix products, arithmetic and copies ran while one was open for 3% of the time, Pallas kernels for 0%

profile of v1, /device:TPU:1, one launch (start us, length us, event | category | flops | bytes accessed | tf_op | source)
XLA Modules:
  0.0 83.3 jit_solution(948556699307284628)
XLA Ops:
  0.0 1.4 %squeeze.6 = bf16[2,64,2,2,4,256]{5,4,3,2,1,0:T(4,128)(2,1)S(1)} reshape(bf16[2,1,1024,256]{3,2,1,0:T(8,128)(2,1)} %param.7) | data formatting | bytes 2097152 | tf_op jit(solution)/shard_map/squeeze | solution.py:40
  1.7 0.5 copy_multiply_fusion
  2.2 0.4 reverse_select_fusion.1
  2.6 0.4 fusion.12
  3.1 0.4 slice_negate_fusion
  3.5 2.0 %maximum_maximum_fusion = bf16[2,2,64,2,4,512]{5,4,3,2,1,0:T(4,128)(2,1)} fusion(bf16[2,2,64,1,4,256]{5,4,3,2,1,0:T(4,128)(2,1)S(1)} %get-tuple-element.6, bf16[2,2,64,1,4,256]{5,4,3,2,1,0:T(4,128)(2,1)S(1)} %get-tuple-element.5, bf16[2,2,64,2,4,256]{5,4,3,2,1,0:T(4,128)(2,1)S(1)} %fusion.12), kind=kLoop, calls=%fused_computation | loop fusion | flops 6291456 | bytes 4194304 | tf_op jit(solution)/shard_map/concatenate | solution.py:47
  5.5 2.5 %reshape.44 = bf16[2,2,512,512]{3,2,1,0:T(8,128)(2,1)S(1)} reshape(bf16[2,2,64,2,4,512]{5,4,3,2,1,0:T(4,128)(2,1)} %maximum_maximum_fusion) | data formatting | bytes 4194304 | tf_op jit(solution)/shard_map/reshape | solution.py:47
  8.1 0.7 convolution_multiply_fusion
  8.9 3.3 %collective-permute-start = (f16[2,512,256]{2,1,0:T(8,128)(2,1)S(1)}, f16[2,512,256]{2,1,0:T(8,128)(2,1)S(1)}, u32[]{:S(2)}, u32[]{:S(2)}) collective-permute-start(f16[2,512,256]{2,1,0:T(8,128)(2,1)S(1)} %fusion.16), channel_id=1, source_target_pairs={{0,1},{1,0},{2,3},{3,2},{4,5},{5,4},{6,7},{7,6},{8,9},{9,8},{10,11... | collective-permute-start | bytes 1572872 | tf_op jit(solution)/shard_map/ppermute | solution.py:52
  12.2 1.5 %collective-permute-done = f16[2,512,256]{2,1,0:T(8,128)(2,1)S(1)} collective-permute-done((f16[2,512,256]{2,1,0:T(8,128)(2,1)S(1)}, f16[2,512,256]{2,1,0:T(8,128)(2,1)S(1)}, u32[]{:S(2)}, u32[]{:S(2)}) %collective-permute-start) | collective-permute-done | bytes 524320 | tf_op jit(solution)/shard_map/ppermute | solution.py:52
  13.9 1.3 %collective-permute-start.1 = (f16[512,256]{1,0:T(8,128)(2,1)S(1)}, f16[512,256]{1,0:T(8,128)(2,1)S(1)}, u32[]{:S(2)}, u32[]{:S(2)}) collective-permute-start(f16[512,256]{1,0:T(8,128)(2,1)S(1)} %fusion.20), channel_id=1, source_target_pairs={{0,2},{1,3},{2,0},{3,1},{4,6},{5,7},{6,4},{7,5},{8,10},{9,11},{10,... | collective-permute-start | bytes 786440 | tf_op jit(solution)/shard_map/ppermute | solution.py:54
  15.1 7.8 %collective-permute-done.1 = f16[512,256]{1,0:T(8,128)(2,1)S(1)} collective-permute-done((f16[512,256]{1,0:T(8,128)(2,1)S(1)}, f16[512,256]{1,0:T(8,128)(2,1)S(1)}, u32[]{:S(2)}, u32[]{:S(2)}) %collective-permute-start.1) | collective-permute-done | bytes 262176 | tf_op jit(solution)/shard_map/ppermute | solution.py:54
  22.9 0.8 fusion.19
  23.7 11.2 %all-to-all-start = ((f16[64,8,256]{2,1,0:T(8,128)(2,1)}), f16[64,8,256]{2,1,0:T(8,128)(2,1)}, u32[]{:S(2)}, u32[]{:S(2)}) async-start(f16[64,8,256]{2,1,0:T(8,128)(2,1)} %fusion.19), calls=%async_computation | async-start | bytes 524288 | tf_op jit(solution)/shard_map/all_to_all | solution.py:57
  35.0 0.2 lt.19
  35.4 9.3 %all-to-all-done = f16[64,8,256]{2,1,0:T(8,128)(2,1)} async-done(((f16[64,8,256]{2,1,0:T(8,128)(2,1)}), f16[64,8,256]{2,1,0:T(8,128)(2,1)}, u32[]{:S(2)}, u32[]{:S(2)}) %all-to-all-start) | async-done | bytes 262176 | tf_op jit(solution)/shard_map/all_to_all | solution.py:57
  44.7 2.3 %convolution_select_fusion = f32[512,256]{1,0:T(8,128)S(1)} fusion(f32[512,512]{1,0:T(8,128)} %constant.37.clone, s32[512,256]{1,0:T(8,128)S(1)} %lt.19, f16[64,8,256]{2,1,0:T(8,128)(2,1)} %all-to-all-done, s32[512]{0:T(512)S(1)} %iota.12), kind=kOutput, calls=%fused_computation.6 | convolution fusion | flops 805568512 | bytes 2361344 | tf_op jit(solution)/shard_map/dot_general | solution.py:24
  47.0 1.9 %fusion.11 = bf16[512,256]{0,1:T(8,128)(2,1)S(1)} fusion(f32[512,256]{1,0:T(8,128)S(1)} %convolution_select_fusion, f32[512,512]{1,0:T(8,128)S(1)} %copy-done.1), kind=kOutput, calls=%fused_computation.11 | convolution fusion | flops 805437440 | bytes 1835008 | tf_op jit(solution)/shard_map/dot_general | solution.py:24
  49.0 17.2 %all_to_all.10 = bf16[64,8,256]{2,1,0:T(8,128)(2,1)S(1)} all-to-all(bf16[64,8,256]{2,1,0:T(8,128)(2,1)S(1)} %bitcast.72), channel_id=1, replica_groups=mesh['freq'=64,'panel'=4] {'freq'}, dimensions={0} | all-to-all | bytes 524288 | tf_op jit(solution)/shard_map/all_to_all | solution.py:68
  66.2 2.6 %collective-permute-start.2 = (bf16[512,256]{1,0:T(8,128)(2,1)S(1)}, bf16[512,256]{1,0:T(8,128)(2,1)S(1)}, u32[]{:S(2)}, u32[]{:S(2)}) collective-permute-start(bf16[512,256]{1,0:T(8,128)(2,1)S(1)} %bitcast.73), channel_id=1, source_target_pairs={{0,2},{1,3},{2,0},{3,1},{4,6},{5,7},{6,4},{7,5},{8,10},{9,11},{10,... | collective-permute-start | bytes 786440 | tf_op jit(solution)/shard_map/ppermute | solution.py:71
  68.8 4.1 %collective-permute-done.2 = bf16[512,256]{1,0:T(8,128)(2,1)S(1)} collective-permute-done((bf16[512,256]{1,0:T(8,128)(2,1)S(1)}, bf16[512,256]{1,0:T(8,128)(2,1)S(1)}, u32[]{:S(2)}, u32[]{:S(2)}) %collective-permute-start.2) | collective-permute-done | bytes 262176 | tf_op jit(solution)/shard_map/ppermute | solution.py:71
  73.0 4.8 %collective-permute-start.3 = (bf16[2,512,256]{2,1,0:T(8,128)(2,1)S(1)}, bf16[2,512,256]{2,1,0:T(8,128)(2,1)}, u32[]{:S(2)}, u32[]{:S(2)}) collective-permute-start(bf16[2,512,256]{2,1,0:T(8,128)(2,1)S(1)} %get-tuple-element.8), channel_id=1, source_target_pairs={{0,1},{1,0},{2,3},{3,2},{4,5},{5,4},{6,7},{7,6},{8,9},{9,8},{10,11... | collective-permute-start | bytes 1572872 | tf_op jit(solution)/shard_map/ppermute | solution.py:72
  77.8 2.0 %reshape.45 = bf16[2,256,2,2,512]{1,0,4,2,3:T(2,128)(2,1)} reshape(bf16[512,2,2,512]{0,3,1,2:T(8,128)(2,1)S(1)} %bitcast.71) | data formatting | bytes 4194304 | tf_op jit(solution)/shard_map/reshape.9
  79.9 3.4 %fusion.8 = f32[2,1,256,256]{3,2,1,0:T(8,128)} fusion(bf16[2,256,2,2,512]{1,0,4,2,3:T(2,128)(2,1)} %reshape.45, bf16[2,1,512,256]{3,2,0,1:T(8,128)(2,1)} %bitcast.19, bf16[2,1,512,256]{3,2,0,1:T(8,128)(2,1)S(1)} %get-tuple-element.7, f32[2,1,256,256]{3,2,1,0:T(8,128)} %param.10), kind=kOutput, calls=%fused_computation.9 | convolution fusion | flops 537526272 | bytes 4194304 | tf_op jit(solution)/shard_map/hcsr,hcsv->rv/dot_general | solution.py:73
  (21 shorter events, 1.0 us)
Async XLA Ops:
  0.0 8.0 %copy-start = (bf16[2,1,256,256]{3,2,1,0:T(8,128)(2,1)S(1)}, bf16[2,1,256,256]{3,2,1,0:T(8,128)(2,1)}, u32[]{:S(2)}) copy-start(bf16[2,1,256,256]{3,2,1,0:T(8,128)(2,1)} %param.9) | copy-start | bytes 786436
  0.0 1.4 %copy-start.3 = (s32[1,16,4]{1,2,0:T(4,128)S(1)}, s32[1,16,4]{1,2,0:T(4,128)}, u32[]{:S(2)}) copy-start(s32[1,16,4]{1,2,0:T(4,128)} %param.8) | copy-start | bytes 772
  8.9 26.1 %copy-start.2 = (s32[4,256]{1,0:T(4,128)S(1)}, s32[4,256]{1,0:T(4,128)}, u32[]{:S(2)}) copy-start(s32[4,256]{1,0:T(4,128)} %param.11) | copy-start | bytes 12292
  8.9 4.8 %collective-permute-start = (f16[2,512,256]{2,1,0:T(8,128)(2,1)S(1)}, f16[2,512,256]{2,1,0:T(8,128)(2,1)S(1)}, u32[]{:S(2)}, u32[]{:S(2)}) collective-permute-start(f16[2,512,256]{2,1,0:T(8,128)(2,1)S(1)} %fusion.16), channel_id=1, source_target_pairs={{0,1},{1,0},{2,3},{3,2},{4,5},{5,4},{6,7},{7,6},{8,9},{9,8},{10,11... | collective-permute-start | bytes 1572872 | tf_op jit(solution)/shard_map/ppermute | solution.py:52
  13.9 9.1 %collective-permute-start.1 = (f16[512,256]{1,0:T(8,128)(2,1)S(1)}, f16[512,256]{1,0:T(8,128)(2,1)S(1)}, u32[]{:S(2)}, u32[]{:S(2)}) collective-permute-start(f16[512,256]{1,0:T(8,128)(2,1)S(1)} %fusion.20), channel_id=1, source_target_pairs={{0,2},{1,3},{2,0},{3,1},{4,6},{5,7},{6,4},{7,5},{8,10},{9,11},{10,... | collective-permute-start | bytes 786440 | tf_op jit(solution)/shard_map/ppermute | solution.py:54
  23.7 21.0 %all-to-all-start = ((f16[64,8,256]{2,1,0:T(8,128)(2,1)}), f16[64,8,256]{2,1,0:T(8,128)(2,1)}, u32[]{:S(2)}, u32[]{:S(2)}) async-start(f16[64,8,256]{2,1,0:T(8,128)(2,1)} %fusion.19), calls=%async_computation | async-start | bytes 524288 | tf_op jit(solution)/shard_map/all_to_all | solution.py:57
  44.7 2.3 %copy-start.1 = (f32[512,512]{1,0:T(8,128)S(1)}, f32[512,512]{1,0:T(8,128)}, u32[]{:S(2)}) copy-start(f32[512,512]{1,0:T(8,128)} %constant.38.clone) | copy-start | bytes 3145732
  66.2 6.8 %collective-permute-start.2 = (bf16[512,256]{1,0:T(8,128)(2,1)S(1)}, bf16[512,256]{1,0:T(8,128)(2,1)S(1)}, u32[]{:S(2)}, u32[]{:S(2)}) collective-permute-start(bf16[512,256]{1,0:T(8,128)(2,1)S(1)} %bitcast.73), channel_id=1, source_target_pairs={{0,2},{1,3},{2,0},{3,1},{4,6},{5,7},{6,4},{7,5},{8,10},{9,11},{10,... | collective-permute-start | bytes 786440 | tf_op jit(solution)/shard_map/ppermute | solution.py:71
  73.0 6.8 %collective-permute-start.3 = (bf16[2,512,256]{2,1,0:T(8,128)(2,1)S(1)}, bf16[2,512,256]{2,1,0:T(8,128)(2,1)}, u32[]{:S(2)}, u32[]{:S(2)}) collective-permute-start(bf16[2,512,256]{2,1,0:T(8,128)(2,1)S(1)} %get-tuple-element.8), channel_id=1, source_target_pairs={{0,1},{1,0},{2,3},{3,2},{4,5},{5,4},{6,7},{7,6},{8,9},{9,8},{10,11... | collective-permute-start | bytes 1572872 | tf_op jit(solution)/shard_map/ppermute | solution.py:72

commit v2 on v1

v2 whole, which is shorter than its diff:
```python
import math

import jax
import jax.numpy as jnp
import numpy as np
from jax import lax
from jax.experimental import pallas as pl
from jax.experimental.pallas import tpu as pltpu
from jax.sharding import PartitionSpec as P

SCALE = 16.0
VMEM = 24 << 20
CORE = ((0, 1), (1, 0), (2, 3), (3, 2))
CHIP = ((0, 2), (1, 3), (2, 0), (3, 1))
F32, BF16, F16 = jnp.float32, jnp.bfloat16, jnp.float16


def transform(length, rows):
    counter = np.arange(length)
    angles = (counter[:, None] * counter[None, :] % length) * (2.0 * math.pi / length)
    cosine, sine = np.cos(angles), np.sin(angles)
    small = np.stack([np.stack([cosine, -sine], -1), np.stack([sine, cosine], -1)], 1)
    full = np.einsum("acbd,jk->acjbdk", small, np.eye(rows))
    full = full.reshape(2 * length * rows, 2 * length * rows).astype(np.float32)
    high = full.astype(BF16)
    return high, (full - high.astype(np.float32)).astype(BF16)


def dot(left, right):
    return jnp.dot(left, right, preferred_element_type=F32)


def masked_rows(operator_ref, mask_ref):
    _, groups, _, eight, columns = operator_ref.shape
    tiles, bands = mask_ref.shape
    lane = lax.broadcasted_iota(jnp.int32, (1, columns), 1) // (columns // tiles)
    keep = []
    for band in range(bands):
        row = jnp.zeros((1, columns), F32)
        for tile in range(tiles):
            row = jnp.where(lane == tile, mask_ref[tile, band].astype(F32), row)
        keep.append(jnp.broadcast_to(row, (groups * eight // bands, columns)).astype(BF16))
    keep = jnp.concatenate(keep, 0)
    return [operator_ref[part, :, 0].reshape(groups * eight, columns) * keep for part in (0, 1)]


def forward_kernel(where_ref, operator_ref, mask_ref, field_ref, out_ref):
    groups, eight, points = out_ref.shape[1:]
    real, imag = masked_rows(operator_ref, mask_ref)
    field_re, field_im = field_ref[0] * SCALE, field_ref[1] * SCALE
    fields = jnp.concatenate(
        [jnp.concatenate([field_re, field_im], 1), jnp.concatenate([-field_im, field_re], 1)], 0
    )
    sums = dot(jnp.concatenate([real, imag], 1), fields)
    real = sums[:, :points].reshape(groups, eight, points)
    imag = sums[:, points:].reshape(groups, eight, points)
    first = lax.broadcasted_iota(jnp.int32, real.shape, 1) < eight // 2
    core = where_ref[1]
    out_ref[core] = jnp.where(first, real, pltpu.roll(imag, eight // 2, axis=1))
    out_ref[1 - core] = jnp.where(first, pltpu.roll(real, eight // 2, axis=1), imag)


def adjoint_kernel(where_ref, operator_ref, mask_ref, own_ref, other_ref, base_ref, out_ref):
    groups, eight, points = own_ref.shape
    columns = operator_ref.shape[-1]
    real, imag = masked_rows(operator_ref, mask_ref)
    own, other = own_ref[...].astype(F32), other_ref[...].astype(F32)
    is_first = where_ref[1] == 0
    low, high = jnp.where(is_first, own, other), jnp.where(is_first, other, own)
    first = lax.broadcasted_iota(jnp.int32, low.shape, 1) < eight // 2
    field_re = jnp.where(first, low, pltpu.roll(high, eight // 2, axis=1))
    field_im = jnp.where(first, pltpu.roll(low, eight // 2, axis=1), high)
    field_re = field_re.reshape(groups * eight, points).astype(BF16)
    field_im = field_im.reshape(groups * eight, points).astype(BF16)
    fields = jnp.concatenate(
        [jnp.concatenate([field_re, field_im], 1), jnp.concatenate([field_im, -field_re], 1)], 0
    )
    sums = lax.dot_general(
        jnp.concatenate([real, imag], 0), fields, (((0,), (0,)), ((), ())), preferred_element_type=F32
    )
    out_ref[:columns] = base_ref[:columns] + sums[:, :points]
    out_ref[columns:] = base_ref[columns:] + sums[:, points:]


def split_dot(high_ref, low_ref, field):
    top = field.astype(BF16)
    rest = (field - top.astype(F32)).astype(BF16)
    high = high_ref[...]
    return dot(high, top) + (dot(low_ref[...], top) + dot(high, rest))


def window_kernel(high_ref, low_ref, traces_ref, onsets_ref, out_ref):
    length, eight, points = out_ref.shape
    shape = (length, eight, points)
    rows = length * eight
    series = split_dot(high_ref, low_ref, traces_ref[...]).reshape(shape)
    onsets = jnp.concatenate([onsets_ref[...]] * 2, 0)
    inside = lax.broadcasted_iota(jnp.int32, shape, 0) < onsets[None]
    sign = jnp.where(lax.broadcasted_iota(jnp.int32, shape, 1) < eight // 2, 1.0, -1.0)
    series = jnp.where(inside, series * (sign * (1.0 / (SCALE * length))), 0.0)
    windowed = split_dot(high_ref, low_ref, series.reshape(rows, points)).reshape(shape)
    out_ref[...] = (windowed * sign).reshape(rows, points).astype(BF16).reshape(shape)


def chosen_rows(operator, half):
    parts, groups, _, eight, columns = operator.shape
    return pl.BlockSpec(
        (parts, groups, 1, eight, columns),
        lambda step, where: (0, 0, where[0] if half == 0 else 1 - where[0], 0, 0),
    )


def whole(array):
    return pl.BlockSpec(array.shape, lambda step, where: (0,) * array.ndim)


SCALARS = pl.BlockSpec(memory_space=pltpu.SMEM)


def call(kernel, name, half, where, operator, mask, others, shape, flops):
    size = math.prod(shape) * 4 + operator.size + sum(o.size * o.dtype.itemsize for o in others)
    return pl.pallas_call(
        kernel,
        name=name,
        grid_spec=pltpu.PrefetchScalarGridSpec(
            num_scalar_prefetch=1,
            grid=(1,),
            in_specs=[chosen_rows(operator, half), SCALARS] + [whole(o) for o in others],
            out_specs=pl.BlockSpec(shape, lambda step, where: (0,) * len(shape)),
        ),
        out_shape=jax.ShapeDtypeStruct(shape, F32),
        cost_estimate=pl.CostEstimate(flops=flops, bytes_accessed=size, transcendentals=0),
        compiler_params=pltpu.CompilerParams(vmem_limit_bytes=VMEM),
    )(where, operator, mask, *others)


def local(reflection, tile_mask, focusing, initial, onsets):
    sources, columns = reflection.shape[2], reflection.shape[3]
    points = focusing.shape[3]
    groups = lax.axis_size("freq")
    rows = sources // groups // lax.axis_size("panel")
    eight = 2 * rows
    panel = lax.axis_index("panel")
    where = jnp.stack([panel >> 1, panel & 1])
    operator = reflection.reshape(2, groups, 2, eight, columns)
    mask = tile_mask[0].T
    fields = focusing[:, 0]
    work = 4 * sources * columns * points

    def forward(half):
        return call(
            forward_kernel, "forward", half, where, operator, mask, [fields],
            (2, groups, eight, points), work,
        )

    def reduce_core(partial):
        return partial[0] + lax.ppermute(partial[1].astype(F16), "panel", CORE).astype(F32)

    away = reduce_core(forward(1))
    arrived = lax.ppermute(away.astype(F16), "panel", CHIP)
    total = reduce_core(forward(0)) + arrived.astype(F32)
    traces = lax.all_to_all(total.astype(F16), "freq", split_axis=0, concat_axis=0, tiled=True)

    high, low = (jnp.asarray(m) for m in transform(groups, rows))
    flat = traces.astype(F32).reshape(groups * eight, points)
    windowed = pl.pallas_call(
        window_kernel,
        name="window",
        out_shape=jax.ShapeDtypeStruct((groups, eight, points), BF16),
        compiler_params=pltpu.CompilerParams(vmem_limit_bytes=VMEM),
    )(high, low, flat, onsets)

    own = lax.all_to_all(windowed, "freq", split_axis=0, concat_axis=0, tiled=True)
    far = lax.ppermute(own, "panel", CHIP)
    own_pair = lax.ppermute(own, "panel", CORE)
    base = initial.reshape(2 * columns, points)

    def adjoint(half, near, partner, base):
        return call(
            adjoint_kernel, "adjoint", half, where, operator, mask, [near, partner, base],
            base.shape, work,
        )

    updated = adjoint(0, own, own_pair, base)
    updated = adjoint(1, far, lax.ppermute(far, "panel", CORE), updated)
    return updated.reshape(initial.shape)


def solution(mesh):
    return jax.shard_map(
        local,
        mesh=mesh,
        in_specs=(
            P(None, "freq", None, "panel"),
            P("freq", None, "panel"),
            P(None, "freq", "panel", None),
            P(None, "freq", "panel", None),
            P(("freq", "panel"), None),
        ),
        out_specs=P(None, "freq", "panel", None),
        check_vma=False,
    )
```

time: 83.5 us -> 75.7 us (0.907)
  blocking collectives: 17.2 us -> 38.1 us
  waiting for transfers between devices: 22.8 us -> 7.96 us
  Pallas kernels: 0 us -> 9.14 us
  matrix products: 8.2 us -> 0 us
  starting transfers between devices: 23.2 us -> 15.9 us
  other arithmetic: 4.82 us -> 0.39 us
  local copies, waits for them, and re-layouts: 6.82 us -> 3.86 us
    all_to_all x1 -> x2, blocking collectives: 17.2 us -> 38.1 us  [the longest x1 20.8 us: local(): lax.all_to_all(total.astype(F16), 'freq', split_axis=0, concat_axis=0, ti...]
    all_to_all x1 -> x0, starting transfers between devices: 11.2 us -> none  [local(): lax.all_to_all(partial.astype(jnp.float16).reshape(groups, 2 * rows, poin...]
    all_to_all x1 -> x0, waiting for transfers between devices: 9.32 us -> none  [local(): lax.all_to_all(partial.astype(jnp.float16).reshape(groups, 2 * rows, poin...]
    pallas_call x0 -> x5, Pallas kernels: none -> 9.14 us  [the longest x4 7.31 us: call(): pl.pallas_call(kernel, name=name, grid_spec=pltpu.PrefetchScalarGridSpec(...]
    dot_general x4 -> x0, matrix products: 8.2 us -> none  [the longest x2 4.12 us: exact_dot(): jnp.dot(left, right, precision=lax.Precision.HIGHEST, preferred_element_t...]
    ppermute x4 -> x6, waiting for transfers between devices: 13.5 us -> 7.96 us  [the longest x1 7.55 us: local(): arrived = lax.ppermute(away.astype(F16), 'panel', CHIP)]
    ppermute x4 -> x6, starting transfers between devices: 12 us -> 15.9 us  [the longest x1 4.69 us: local(): updated = adjoint(1, far, lax.ppermute(far, 'panel', CORE), updated)]
    unnamed x8 -> x16, local copies, waits for them, and re-layouts: 0.02 us -> 3.86 us
  transfers between devices with their start and end apart: 5 -> 6, of which waited for: 4 -> 3; matrix products, arithmetic and copies ran while one was open for 3% -> 0% of each run, Pallas kernels for 0% -> 4%
where the time goes in v2:
time: 75.7 us; the launch traced here: 75.4 us
  blocking collectives  38.1 us (50%)
  starting transfers between devices  15.9 us (21%)
  Pallas kernels  9.14 us (12%)
  waiting for transfers between devices  7.96 us (11%)
  local copies, waits for them, and re-layouts  3.86 us (5%)
    all_to_all x1, blocking collectives, local(): lax.all_to_all(total.astype(F16), 'freq', split_axis=0, concat_axis=0, ti...  20.8 us
    all_to_all x1, blocking collectives, local(): lax.all_to_all(windowed, 'freq', split_axis=0, concat_axis=0, tiled=True)  17.3 us
    ppermute x1, waiting for transfers between devices, local(): arrived = lax.ppermute(away.astype(F16), 'panel', CHIP)  7.55 us
    pallas_call x4, Pallas kernels, call(): pl.pallas_call(kernel, name=name, grid_spec=pltpu.PrefetchScalarGridSpec(...  7.31 us
    ppermute x1, starting transfers between devices, local(): updated = adjoint(1, far, lax.ppermute(far, 'panel', CORE), updated)  4.69 us
    ppermute x1, starting transfers between devices, local(): own_pair = lax.ppermute(own, 'panel', CORE)  3.87 us
    unnamed x16, local copies, waits for them, and re-layouts  3.86 us
    ppermute x2, starting transfers between devices, reduce_core(): lax.ppermute(partial[1].astype(F16), 'panel', CORE).astype(F32)  3.39 us
  transfers between devices with their start and end apart: 6, of which 3 were waited for; matrix products, arithmetic and copies ran while one was open for 0% of the time, Pallas kernels for 4%

profile of v2, /device:TPU:1, one launch (start us, length us, event | category | flops | bytes accessed | tf_op | source)
XLA Modules:
  0.0 75.4 jit_solution(11930129780057491114)
XLA Ops:
  0.0 0.1 pad_add_fusion.where_ref
  0.1 0.7 copy-done.6
  0.8 1.2 %copy-done = bf16[2,1,1024,256]{3,2,1,0:T(8,128)(2,1)S(1)} copy-done((bf16[2,1,1024,256]{3,2,1,0:T(8,128)(2,1)S(1)}, bf16[2,1,1024,256]{3,2,1,0:T(8,128)(2,1)}, u32[]{:S(2)}) %copy-start) | copy-done | bytes 1048600
  2.0 0.9 %copy-done.2 = bf16[2,1,256,256]{3,2,1,0:T(8,128)(2,1)S(1)} copy-done((bf16[2,1,256,256]{3,2,1,0:T(8,128)(2,1)S(1)}, bf16[2,1,256,256]{3,2,1,0:T(8,128)(2,1)}, u32[]{:S(2)}) %copy-start.2) | copy-done | bytes 262168
  2.9 1.6 %forward.3 = f32[2,64,8,256]{3,2,1,0:T(8,128)S(1)} custom-call(s32[2]{0:T(128)S(1)} %pad_add_fusion.where_ref, bf16[2,64,2,8,256]{4,3,2,1,0:T(8,128)(2,1)S(1)} %bitcast.32, s32[4,16]{1,0:T(4,128)S(1)} %bitcast.39, bf16[2,256,256]{2,1,0:T(8,128)(2,1)S(1)} %bitcast.36), custom_call_target="tpu_custom_call" | custom-call | flops 268435456 | bytes 1835008 | tf_op jit(solution)/shard_map/forward/pallas_call | solution.py:122
  4.6 3.3 %collective-permute-start.1 = (f16[64,8,256]{2,1,0:T(8,128)(2,1)S(1)}, f16[64,8,256]{2,1,0:T(8,128)(2,1)S(1)}, u32[]{:S(2)}, u32[]{:S(2)}) collective-permute-start(f16[64,8,256]{2,1,0:T(8,128)(2,1)S(1)} %fusion.6), channel_id=1, source_target_pairs={{0,1},{1,0},{2,3},{3,2},{4,5},{5,4},{6,7},{7,6},{8,9},{9,8},{10,11... | collective-permute-start | bytes 786440 | tf_op jit(solution)/shard_map/ppermute | solution.py:157
  7.9 1.6 %forward.2 = f32[2,64,8,256]{3,2,1,0:T(8,128)S(1)} custom-call(s32[2]{0:T(128)S(1)} %pad_add_fusion.where_ref, bf16[2,64,2,8,256]{4,3,2,1,0:T(8,128)(2,1)S(1)} %bitcast.33, s32[4,16]{1,0:T(4,128)S(1)} %bitcast.40, bf16[2,256,256]{2,1,0:T(8,128)(2,1)S(1)} %bitcast.37), custom_call_target="tpu_custom_call" | custom-call | flops 268435456 | bytes 1835008 | tf_op jit(solution)/shard_map/forward/pallas_call | solution.py:122
  9.5 0.1 collective-permute-start
  9.6 0.1 fusion.1
  9.7 1.3 %collective-permute-start.2 = (f16[64,8,256]{2,1,0:T(8,128)(2,1)S(1)}, f16[64,8,256]{2,1,0:T(8,128)(2,1)S(1)}, u32[]{:S(2)}, u32[]{:S(2)}) collective-permute-start(f16[64,8,256]{2,1,0:T(8,128)(2,1)S(1)} %fusion.1), channel_id=1, source_target_pairs={{0,2},{1,3},{2,0},{3,1},{4,6},{5,7},{6,4},{7,5},{8,10},{9,11},{10,... | collective-permute-start | bytes 786440 | tf_op jit(solution)/shard_map/ppermute | solution.py:160
  11.0 0.1 collective-permute-done
  11.1 7.5 %collective-permute-done.2 = f16[64,8,256]{2,1,0:T(8,128)(2,1)S(1)} collective-permute-done((f16[64,8,256]{2,1,0:T(8,128)(2,1)S(1)}, f16[64,8,256]{2,1,0:T(8,128)(2,1)S(1)}, u32[]{:S(2)}, u32[]{:S(2)}) %collective-permute-start.2) | collective-permute-done | bytes 262176 | tf_op jit(solution)/shard_map/ppermute | solution.py:160
  18.7 0.1 fusion.4
  18.8 0.0 copy-start.5
  18.8 20.8 %all_to_all.10 = f16[64,8,256]{2,1,0:T(8,128)(2,1)S(1)} all-to-all(f16[64,8,256]{2,1,0:T(8,128)(2,1)S(1)} %fusion.4), channel_id=1, replica_groups=mesh['freq'=64,'panel'=4] {'freq'}, dimensions={0} | all-to-all | bytes 524288 | tf_op jit(solution)/shard_map/all_to_all | solution.py:162
  39.7 1.0 %copy-done.4 = bf16[512,512]{1,0:T(8,128)(2,1)S(1)} copy-done((bf16[512,512]{1,0:T(8,128)(2,1)S(1)}, bf16[512,512]{1,0:T(8,128)(2,1)}, u32[]{:S(2)}) %copy-start.4) | copy-done | bytes 524312
  40.6 1.8 %window.1 = bf16[64,8,256]{2,1,0:T(8,128)(2,1)S(1)} custom-call(bf16[512,512]{1,0:T(8,128)(2,1)S(1)} %copy-done.5, bf16[512,512]{1,0:T(8,128)(2,1)S(1)} %copy-done.4, f32[512,256]{1,0:T(8,128)S(1)} %bitcast_convert_fusion.traces_ref, s32[4,256]{1,0:T(4,128)S(1)} %copy-done.7), custom_call_target="tpu_custom_call" | custom-call | tf_op jit(solution)/shard_map/window/pallas_call | solution.py:166
  42.5 17.3 %all_to_all.11.own_ref = bf16[64,8,256]{2,1,0:T(8,128)(2,1)S(1)} all-to-all(bf16[64,8,256]{2,1,0:T(8,128)(2,1)S(1)} %window.1), channel_id=1, replica_groups=mesh['freq'=64,'panel'=4] {'freq'}, dimensions={0} | all-to-all | bytes 524288 | tf_op jit(solution)/shard_map/all_to_all | solution.py:173
  59.7 2.6 %collective-permute-start.3 = (bf16[64,8,256]{2,1,0:T(8,128)(2,1)S(1)}, bf16[64,8,256]{2,1,0:T(8,128)(2,1)S(1)}, u32[]{:S(2)}, u32[]{:S(2)}) collective-permute-start(bf16[64,8,256]{2,1,0:T(8,128)(2,1)S(1)} %all_to_all.11.own_ref), channel_id=1, source_target_pairs={{0,2},{1,3},{2,0},{3,1},{4,6},{5,7},{6,4},{7,5},{8,10},{9,11},{10,... | collective-permute-start | bytes 786440 | tf_op jit(solution)/shard_map/ppermute | solution.py:174
  62.4 3.9 %collective-permute-start.5 = (bf16[64,8,256]{2,1,0:T(8,128)(2,1)S(1)}, bf16[64,8,256]{2,1,0:T(8,128)(2,1)S(1)}, u32[]{:S(2)}, u32[]{:S(2)}) collective-permute-start(bf16[64,8,256]{2,1,0:T(8,128)(2,1)S(1)} %all_to_all.11.own_ref), channel_id=1, source_target_pairs={{0,1},{1,0},{2,3},{3,2},{4,5},{5,4},{6,7},{7,6},{8,9},{9,8},{10,11... | collective-permute-start | bytes 786440 | tf_op jit(solution)/shard_map/ppermute | solution.py:175
  66.2 0.3 collective-permute-done.3.own_ref
  66.5 4.7 %collective-permute-start.4 = (bf16[64,8,256]{2,1,0:T(8,128)(2,1)S(1)}, bf16[64,8,256]{2,1,0:T(8,128)(2,1)S(1)}, u32[]{:S(2)}, u32[]{:S(2)}) collective-permute-start(bf16[64,8,256]{2,1,0:T(8,128)(2,1)S(1)} %collective-permute-done.3.own_ref), channel_id=1, source_target_pairs={{0,1},{1,0},{2,3},{3,2},{4,5},{5,4},{6,7},{7,6},{8,9},{9,8},{10,11... | collective-permute-start | bytes 786440 | tf_op jit(solution)/shard_map/ppermute | solution.py:185
  71.2 1.7 %adjoint.2.base_ref = f32[512,256]{1,0:T(8,128)S(1)} custom-call(s32[2]{0:T(128)S(1)} %pad_add_fusion.where_ref, bf16[2,64,2,8,256]{4,3,2,1,0:T(8,128)(2,1)S(1)} %bitcast.34, s32[4,16]{1,0:T(4,128)S(1)} %bitcast.41, bf16[64,8,256]{2,1,0:T(8,128)(2,1)S(1)} %all_to_all.11.own_ref, bf16[64,8,256]{2,1,0:T(8,128)(2,1)S(1)} %collective-permute-done.5.other_ref, ...), custom_call_target="tpu_custom_call" | custom-call | flops 268435456 | bytes 2097152 | tf_op jit(solution)/shard_map/adjoint/pallas_call | solution.py:122
  72.9 2.5 %adjoint.3 = f32[512,256]{1,0:T(8,128)} custom-call(s32[2]{0:T(128)S(1)} %pad_add_fusion.where_ref, bf16[2,64,2,8,256]{4,3,2,1,0:T(8,128)(2,1)S(1)} %bitcast.35, s32[4,16]{1,0:T(4,128)S(1)} %bitcast.42, bf16[64,8,256]{2,1,0:T(8,128)(2,1)S(1)} %collective-permute-done.3.own_ref, bf16[64,8,256]{2,1,0:T(8,128)(2,1)S(1)} %collective-permute-done.4.other_ref, ...), custom_call_target="tpu_custom_call" | custom-call | flops 268435456 | bytes 2097152 | tf_op jit(solution)/shard_map/adjoint/pallas_call | solution.py:122
  (17 shorter events, 0.1 us)
Async XLA Ops:
  0.1 0.7 copy-start.6
  0.8 1.2 %copy-start = (bf16[2,1,1024,256]{3,2,1,0:T(8,128)(2,1)S(1)}, bf16[2,1,1024,256]{3,2,1,0:T(8,128)(2,1)}, u32[]{:S(2)}) copy-start(bf16[2,1,1024,256]{3,2,1,0:T(8,128)(2,1)} %param.7) | copy-start | bytes 3145732
  2.0 0.9 %copy-start.2 = (bf16[2,1,256,256]{3,2,1,0:T(8,128)(2,1)S(1)}, bf16[2,1,256,256]{3,2,1,0:T(8,128)(2,1)}, u32[]{:S(2)}) copy-start(bf16[2,1,256,256]{3,2,1,0:T(8,128)(2,1)} %param.9) | copy-start | bytes 786436
  4.6 5.0 %collective-permute-start.1 = (f16[64,8,256]{2,1,0:T(8,128)(2,1)S(1)}, f16[64,8,256]{2,1,0:T(8,128)(2,1)S(1)}, u32[]{:S(2)}, u32[]{:S(2)}) collective-permute-start(f16[64,8,256]{2,1,0:T(8,128)(2,1)S(1)} %fusion.6), channel_id=1, source_target_pairs={{0,1},{1,0},{2,3},{3,2},{4,5},{5,4},{6,7},{7,6},{8,9},{9,8},{10,11... | collective-permute-start | bytes 786440 | tf_op jit(solution)/shard_map/ppermute | solution.py:157
  9.5 1.6 %collective-permute-start = (f16[64,8,256]{2,1,0:T(8,128)(2,1)S(1)}, f16[64,8,256]{2,1,0:T(8,128)(2,1)S(1)}, u32[]{:S(2)}, u32[]{:S(2)}) collective-permute-start(f16[64,8,256]{2,1,0:T(8,128)(2,1)S(1)} %fusion.5), channel_id=1, source_target_pairs={{0,1},{1,0},{2,3},{3,2},{4,5},{5,4},{6,7},{7,6},{8,9},{9,8},{10,11... | collective-permute-start | bytes 786440 | tf_op jit(solution)/shard_map/ppermute | solution.py:157
  9.7 9.0 %collective-permute-start.2 = (f16[64,8,256]{2,1,0:T(8,128)(2,1)S(1)}, f16[64,8,256]{2,1,0:T(8,128)(2,1)S(1)}, u32[]{:S(2)}, u32[]{:S(2)}) collective-permute-start(f16[64,8,256]{2,1,0:T(8,128)(2,1)S(1)} %fusion.1), channel_id=1, source_target_pairs={{0,2},{1,3},{2,0},{3,1},{4,6},{5,7},{6,4},{7,5},{8,10},{9,11},{10,... | collective-permute-start | bytes 786440 | tf_op jit(solution)/shard_map/ppermute | solution.py:160
  18.8 20.9 %copy-start.5 = (bf16[512,512]{1,0:T(8,128)(2,1)S(1)}, bf16[512,512]{1,0:T(8,128)(2,1)}, u32[]{:S(2)}) copy-start(bf16[512,512]{1,0:T(8,128)(2,1)} %constant.10.clone.high_ref) | copy-start | bytes 1572868
  39.6 1.0 %copy-start.4 = (bf16[512,512]{1,0:T(8,128)(2,1)S(1)}, bf16[512,512]{1,0:T(8,128)(2,1)}, u32[]{:S(2)}) copy-start(bf16[512,512]{1,0:T(8,128)(2,1)} %constant.11.clone.low_ref) | copy-start | bytes 1572868
  39.6 1.0 %copy-start.7 = (s32[4,256]{1,0:T(4,128)S(1)}, s32[4,256]{1,0:T(4,128)}, u32[]{:S(2)}) copy-start(s32[4,256]{1,0:T(4,128)} %onsets_ref.1) | copy-start | bytes 12292
  40.6 30.6 %copy-start.1 = (bf16[2,1,1024,256]{3,2,1,0:T(8,128)(2,1)S(1)}, bf16[2,1,1024,256]{3,2,1,0:T(8,128)(2,1)}, u32[]{:S(2)}) copy-start(bf16[2,1,1024,256]{3,2,1,0:T(8,128)(2,1)} %param.7) | copy-start | bytes 3145732
  42.5 28.7 %copy-start.3 = (f32[2,1,256,256]{3,2,1,0:T(8,128)S(1)}, f32[2,1,256,256]{3,2,1,0:T(8,128)}, u32[]{:S(2)}) copy-start(f32[2,1,256,256]{3,2,1,0:T(8,128)} %param.10) | copy-start | bytes 1572868
  59.7 6.8 %collective-permute-start.3 = (bf16[64,8,256]{2,1,0:T(8,128)(2,1)S(1)}, bf16[64,8,256]{2,1,0:T(8,128)(2,1)S(1)}, u32[]{:S(2)}, u32[]{:S(2)}) collective-permute-start(bf16[64,8,256]{2,1,0:T(8,128)(2,1)S(1)} %all_to_all.11.own_ref), channel_id=1, source_target_pairs={{0,2},{1,3},{2,0},{3,1},{4,6},{5,7},{6,4},{7,5},{8,10},{9,11},{10,... | collective-permute-start | bytes 786440 | tf_op jit(solution)/shard_map/ppermute | solution.py:174
  62.4 8.8 %collective-permute-start.5 = (bf16[64,8,256]{2,1,0:T(8,128)(2,1)S(1)}, bf16[64,8,256]{2,1,0:T(8,128)(2,1)S(1)}, u32[]{:S(2)}, u32[]{:S(2)}) collective-permute-start(bf16[64,8,256]{2,1,0:T(8,128)(2,1)S(1)} %all_to_all.11.own_ref), channel_id=1, source_target_pairs={{0,1},{1,0},{2,3},{3,2},{4,5},{5,4},{6,7},{7,6},{8,9},{9,8},{10,11... | collective-permute-start | bytes 786440 | tf_op jit(solution)/shard_map/ppermute | solution.py:175
  66.5 6.4 %collective-permute-start.4 = (bf16[64,8,256]{2,1,0:T(8,128)(2,1)S(1)}, bf16[64,8,256]{2,1,0:T(8,128)(2,1)S(1)}, u32[]{:S(2)}, u32[]{:S(2)}) collective-permute-start(bf16[64,8,256]{2,1,0:T(8,128)(2,1)S(1)} %collective-permute-done.3.own_ref), channel_id=1, source_target_pairs={{0,1},{1,0},{2,3},{3,2},{4,5},{5,4},{6,7},{7,6},{8,9},{9,8},{10,11... | collective-permute-start | bytes 786440 | tf_op jit(solution)/shard_map/ppermute | solution.py:185

commit v3 on v2

v3 whole, which is shorter than its diff:
```python
import functools
import math

import jax
import jax.numpy as jnp
import numpy as np
from jax import lax
from jax.experimental import pallas as pl
from jax.experimental.pallas import tpu as pltpu
from jax.sharding import PartitionSpec as P

SCALE = 16.0
VMEM = 24 << 20
CORE = ((0, 1), (1, 0), (2, 3), (3, 2))
CHIP = ((0, 2), (1, 3), (2, 0), (3, 1))
F32, BF16, F16 = jnp.float32, jnp.bfloat16, jnp.float16


def transform(length, rows):
    counter = np.arange(length)
    angles = (counter[:, None] * counter[None, :] % length) * (2.0 * math.pi / length)
    cosine, sine = np.cos(angles), np.sin(angles)
    small = np.stack([np.stack([cosine, -sine], -1), np.stack([sine, cosine], -1)], 1)
    full = np.einsum("acbd,jk->acjbdk", small, np.eye(rows))
    full = full.reshape(2 * length * rows, 2 * length * rows).astype(np.float32)
    high = full.astype(BF16)
    return np.stack([high, (full - high.astype(np.float32)).astype(BF16)])


def dot(left, right):
    return jnp.dot(left, right, preferred_element_type=F32)


def position():
    panel = lax.axis_index("panel")
    return panel >> 1, panel & 1


def masked_rows(rows_ref, mask_ref):
    groups, eight, columns = rows_ref.shape[1:]
    tiles, bands = mask_ref.shape
    lane = lax.broadcasted_iota(jnp.int32, (1, columns), 1) // (columns // tiles)
    keep = []
    for band in range(bands):
        row = jnp.zeros((1, columns), F32)
        for tile in range(tiles):
            row = jnp.where(lane == tile, mask_ref[tile, band].astype(F32), row)
        keep.append(jnp.broadcast_to(row, (groups * eight // bands, columns)).astype(BF16))
    keep = jnp.concatenate(keep, 0)
    return [rows_ref[part].reshape(groups * eight, columns) * keep for part in (0, 1)]


def forward_kernel(
    away, operator_ref, mask_ref, field_ref, out_ref, rows_ref, fields_ref, tiles_ref, sems
):
    groups, eight, points = out_ref.shape[1:]
    chip, core = position()
    half = 1 - chip if away else chip
    copies = [
        pltpu.make_async_copy(mask_ref, tiles_ref, sems.at[0]),
        pltpu.make_async_copy(operator_ref.at[0, :, half], rows_ref.at[0], sems.at[1]),
        pltpu.make_async_copy(operator_ref.at[1, :, half], rows_ref.at[1], sems.at[2]),
        pltpu.make_async_copy(field_ref, fields_ref, sems.at[3]),
    ]
    for copy in copies:
        copy.start()
    for copy in copies:
        copy.wait()
    real, imag = masked_rows(rows_ref, tiles_ref)
    field_re, field_im = fields_ref[0] * SCALE, fields_ref[1] * SCALE
    fields = jnp.concatenate(
        [jnp.concatenate([field_re, field_im], 1), jnp.concatenate([-field_im, field_re], 1)], 0
    )
    sums = dot(jnp.concatenate([real, imag], 1), fields)
    real = sums[:, :points].reshape(groups, eight, points)
    imag = sums[:, points:].reshape(groups, eight, points)
    first = lax.broadcasted_iota(jnp.int32, real.shape, 1) < eight // 2
    out_ref[core] = jnp.where(first, real, pltpu.roll(imag, eight // 2, axis=1))
    out_ref[1 - core] = jnp.where(first, pltpu.roll(real, eight // 2, axis=1), imag)


def ordered_fields(own_ref, other_ref):
    groups, eight, points = own_ref.shape
    own, other = own_ref[...].astype(F32), other_ref[...].astype(F32)
    is_first = position()[1] == 0
    low, high = jnp.where(is_first, own, other), jnp.where(is_first, other, own)
    first = lax.broadcasted_iota(jnp.int32, low.shape, 1) < eight // 2
    field_re = jnp.where(first, low, pltpu.roll(high, eight // 2, axis=1))
    field_im = jnp.where(first, pltpu.roll(low, eight // 2, axis=1), high)
    field_re = field_re.reshape(groups * eight, points).astype(BF16)
    field_im = field_im.reshape(groups * eight, points).astype(BF16)
    return jnp.concatenate(
        [jnp.concatenate([field_re, field_im], 1), jnp.concatenate([field_im, -field_re], 1)], 0
    )


def near_kernel(
    operator_ref, mask_ref, own_ref, other_ref, initial_ref, out_ref, far_ref,
    rows_ref, base_ref, tiles_ref, sems,
):
    columns, points = operator_ref.shape[-1], own_ref.shape[-1]
    chip, _ = position()
    copies = [
        pltpu.make_async_copy(mask_ref, tiles_ref, sems.at[0]),
        pltpu.make_async_copy(operator_ref.at[:, :, chip], rows_ref.at[0], sems.at[1]),
        pltpu.make_async_copy(operator_ref.at[:, :, 1 - chip], rows_ref.at[1], sems.at[2]),
        pltpu.make_async_copy(initial_ref, base_ref, sems.at[3]),
    ]
    for copy in copies:
        copy.start()
    for copy in copies:
        copy.wait()
    near, far = (jnp.concatenate(masked_rows(rows_ref.at[k], tiles_ref), 0) for k in (0, 1))
    far_ref[...] = far.T
    sums = lax.dot_general(
        near, ordered_fields(own_ref, other_ref), (((0,), (0,)), ((), ())),
        preferred_element_type=F32,
    )
    out_ref[:columns] = base_ref[:columns] + sums[:, :points]
    out_ref[columns:] = base_ref[columns:] + sums[:, points:]


def add_far(far_ref, own_ref, other_ref, base_ref, out_ref, lanes):
    columns, points = far_ref.shape[0], own_ref.shape[-1]
    sums = dot(far_ref[...], ordered_fields(own_ref, other_ref))
    out_ref[:columns] = base_ref[:columns, lanes] + sums[:, :points]
    out_ref[columns:] = base_ref[columns:, lanes] + sums[:, points:]


def middle_kernel(far_ref, own_ref, other_ref, base_ref, out_ref):
    add_far(far_ref, own_ref, other_ref, base_ref, out_ref, slice(0, own_ref.shape[-1]))


def last_kernel(far_ref, own_ref, other_ref, base_ref, done_ref, out_ref, rest_ref, sems):
    points = own_ref.shape[-1]
    early = pltpu.make_async_copy(done_ref, out_ref.at[:, :points], sems.at[0])
    early.start()
    add_far(far_ref, own_ref, other_ref, base_ref, rest_ref, slice(points, 2 * points))
    late = pltpu.make_async_copy(rest_ref, out_ref.at[:, points:], sems.at[1])
    late.start()
    early.wait()
    late.wait()


def split_dot(pair_ref, field):
    top = field.astype(BF16)
    rest = (field - top.astype(F32)).astype(BF16)
    high = pair_ref[0]
    return dot(high, top) + (dot(pair_ref[1], top) + dot(high, rest))


def window_kernel(pair_ref, traces_ref, onsets_ref, out_ref):
    length, eight, points = out_ref.shape
    shape = (length, eight, points)
    rows = length * eight
    series = split_dot(pair_ref, traces_ref[...]).reshape(shape)
    onsets = jnp.concatenate([onsets_ref[...]] * 2, 0)
    inside = lax.broadcasted_iota(jnp.int32, shape, 0) < onsets[None]
    sign = jnp.where(lax.broadcasted_iota(jnp.int32, shape, 1) < eight // 2, 1.0, -1.0)
    series = jnp.where(inside, series * (sign * (1.0 / (SCALE * length))), 0.0)
    windowed = split_dot(pair_ref, series.reshape(rows, points)).reshape(shape)
    out_ref[...] = (windowed * sign).reshape(rows, points).astype(BF16).reshape(shape)


HERE = pl.BlockSpec(memory_space=pltpu.HBM)
NEAR = pl.BlockSpec(memory_space=pltpu.VMEM)


def call(kernel, name, ins, outs, scratch, args, flops):
    size = sum(math.prod(o.shape) * o.dtype.itemsize for o in [*args, *(s for _, s in outs)])
    args = [pltpu.with_memory_space_constraint(a, pltpu.HBM) if s is HERE else a for s, a in zip(ins, args)]
    made = pl.pallas_call(
        kernel,
        name=name,
        in_specs=ins,
        out_specs=[spec for spec, _ in outs],
        out_shape=[shape for _, shape in outs],
        scratch_shapes=scratch,
        cost_estimate=pl.CostEstimate(flops=flops, bytes_accessed=size, transcendentals=0),
        compiler_params=pltpu.CompilerParams(vmem_limit_bytes=VMEM),
    )(*args)
    return made if len(outs) > 1 else made[0]


def local(reflection, tile_mask, focusing, initial, onsets):
    sources, columns = reflection.shape[2], reflection.shape[3]
    points = focusing.shape[3]
    groups = lax.axis_size("freq")
    rows = sources // groups // lax.axis_size("panel")
    eight = 2 * rows
    operator = reflection.reshape(2, groups, 2, eight, columns)
    mask = tile_mask[0].T
    fields = focusing[:, 0]
    work = 4 * sources * columns * points
    shaped = jax.ShapeDtypeStruct
    tiles = pltpu.SMEM(mask.shape, jnp.int32)
    sems = pltpu.SemaphoreType.DMA((4,))
    rows_shape = (2, groups, eight, columns)

    def forward(away, fields):
        return call(
            functools.partial(forward_kernel, away), "forward", [HERE] * 3,
            [(NEAR, shaped((2, groups, eight, points), F32))],
            [pltpu.VMEM(rows_shape, BF16), pltpu.VMEM(fields.shape, BF16), tiles, sems],
            [operator, mask, fields], work,
        )

    def swap(array, pairs):
        return lax.ppermute(array, "panel", pairs)

    away = forward(True, fields)
    away = (away[0] + swap(away[1].astype(F16), CORE).astype(F32)).astype(F16)
    away, fields = lax.optimization_barrier((away, fields))
    total = forward(False, fields)
    arrived = swap(away, CHIP)
    total = total[0] + swap(total[1].astype(F16), CORE).astype(F32) + arrived.astype(F32)
    traces = lax.all_to_all(total.astype(F16), "freq", split_axis=0, concat_axis=0, tiled=True)

    pair = jnp.asarray(transform(groups, rows))
    flat = traces.astype(F32).reshape(groups * eight, points)
    windowed = call(
        window_kernel, "window", [NEAR] * 3, [(NEAR, shaped(traces.shape, BF16))], [],
        [pair, flat, onsets], 12 * flat.shape[0] ** 2 * points,
    )

    own = lax.all_to_all(windowed, "freq", split_axis=0, concat_axis=0, tiled=True)
    cut = points // 2
    far = [swap(own[:, :, :cut], CHIP), swap(own[:, :, cut:], CHIP)]
    base = shaped((2 * columns, points), F32)
    updated, turned = call(
        near_kernel, "near", [HERE] * 2 + [NEAR] * 2 + [HERE],
        [(NEAR, base), (NEAR, shaped((columns, sources), BF16))],
        [pltpu.VMEM((2, *rows_shape), BF16), pltpu.VMEM(base.shape, F32), tiles, sems],
        [operator, mask, own, swap(own, CORE), initial.reshape(base.shape)], work,
    )
    far[0], updated = lax.optimization_barrier((far[0], updated))
    done = call(
        middle_kernel, "middle", [NEAR] * 4, [(NEAR, shaped((2 * columns, cut), F32))], [],
        [turned, far[0], swap(far[0], CORE), updated], work // 2,
    )
    updated = call(
        last_kernel, "last", [NEAR] * 5, [(HERE, base)],
        [pltpu.VMEM((2 * columns, points - cut), F32), pltpu.SemaphoreType.DMA((2,))],
        [turned, far[1], swap(far[1], CORE), updated, done], work // 2,
    )
    return updated.reshape(initial.shape)


def solution(mesh):
    return jax.shard_map(
        local,
        mesh=mesh,
        in_specs=(
            P(None, "freq", None, "panel"),
            P("freq", None, "panel"),
            P(None, "freq", "panel", None),
            P(None, "freq", "panel", None),
            P(("freq", "panel"), None),
        ),
        out_specs=P(None, "freq", "panel", None),
        check_vma=False,
    )
```

time: 75.7 us -> 72 us (0.951)
  local copies, waits for them, and re-layouts: 3.86 us -> 0.66 us
  waiting for transfers between devices: 7.96 us -> 10.5 us
  starting transfers between devices: 15.9 us -> 14 us
  Pallas kernels: 9.14 us -> 8.36 us
    unnamed x16 -> x4, local copies, waits for them, and re-layouts: 3.86 us -> 0.64 us
    ppermute x6 -> x8, waiting for transfers between devices: 7.96 us -> 10.5 us  [swap(): return lax.ppermute(array, 'panel', pairs)]
    ppermute x6 -> x8, starting transfers between devices: 15.9 us -> 14 us  [swap(): return lax.ppermute(array, 'panel', pairs)]
    pallas_call x5 -> x6, Pallas kernels: 9.14 us -> 8.36 us  [call(): pl.pallas_call(kernel, name=name, in_specs=ins, out_specs=[spec for spec,...]
  transfers between devices with their start and end apart: 6 -> 8, of which waited for: 3 -> 5; matrix products, arithmetic and copies ran while one was open for 0% -> 0% of each run, Pallas kernels for 4% -> 5%
where the time goes in v3:
time: 72 us; the launch traced here: 71.7 us
  blocking collectives  37.9 us (53%)
  starting transfers between devices  14 us (19%)
  waiting for transfers between devices  10.5 us (15%)
  Pallas kernels  8.36 us (12%)
    all_to_all x1, blocking collectives, local(): lax.all_to_all(total.astype(F16), 'freq', split_axis=0, concat_axis=0, ti...  20.7 us
    all_to_all x1, blocking collectives, local(): lax.all_to_all(windowed, 'freq', split_axis=0, concat_axis=0, tiled=True)  17.2 us
    ppermute x8, starting transfers between devices, swap(): return lax.ppermute(array, 'panel', pairs)  14 us
    ppermute x8, waiting for transfers between devices, swap(): return lax.ppermute(array, 'panel', pairs)  10.5 us
    pallas_call x6, Pallas kernels, call(): pl.pallas_call(kernel, name=name, in_specs=ins, out_specs=[spec for spec,...  8.36 us
  transfers between devices with their start and end apart: 8, of which 5 were waited for; matrix products, arithmetic and copies ran while one was open for 0% of the time, Pallas kernels for 5%

profile of v3, /device:TPU:1, one launch (start us, length us, event | category | flops | bytes accessed | tf_op | source)
XLA Modules:
  0.0 71.7 jit_solution(11660028848275227744)
XLA Ops:
  0.0 1.6 %forward.2 = f32[2,64,8,256]{3,2,1,0:T(8,128)S(1)} custom-call(bf16[2,64,2,8,256]{4,3,2,1,0:T(8,128)(2,1)} %bitcast.30, s32[4,16]{1,0:T(4,128)} %bitcast.36, bf16[2,256,256]{2,1,0:T(8,128)(2,1)} %bitcast.33), custom_call_target="tpu_custom_call" | custom-call | flops 268435456 | bytes 2359552 | tf_op jit(solution)/shard_map/forward/pallas_call | solution.py:172
  1.6 3.3 %collective-permute-start = (f16[64,8,256]{2,1,0:T(8,128)(2,1)S(1)}, f16[64,8,256]{2,1,0:T(8,128)(2,1)S(1)}, u32[]{:S(2)}, u32[]{:S(2)}) collective-permute-start(f16[64,8,256]{2,1,0:T(8,128)(2,1)S(1)} %fusion.5), channel_id=1, source_target_pairs={{0,1},{1,0},{2,3},{3,2},{4,5},{5,4},{6,7},{7,6},{8,9},{9,8},{10,11... | collective-permute-start | bytes 786440 | tf_op jit(solution)/shard_map/ppermute | solution.py:209
  4.9 1.2 %collective-permute-done = f16[64,8,256]{2,1,0:T(8,128)(2,1)S(1)} collective-permute-done((f16[64,8,256]{2,1,0:T(8,128)(2,1)S(1)}, f16[64,8,256]{2,1,0:T(8,128)(2,1)S(1)}, u32[]{:S(2)}, u32[]{:S(2)}) %collective-permute-start) | collective-permute-done | bytes 262176 | tf_op jit(solution)/shard_map/ppermute | solution.py:209
  6.1 0.1 fusion.4
  6.2 1.3 %collective-permute-start.2 = (f16[64,8,256]{2,1,0:T(8,128)(2,1)S(1)}, f16[64,8,256]{2,1,0:T(8,128)(2,1)S(1)}, u32[]{:S(2)}, u32[]{:S(2)}) collective-permute-start(f16[64,8,256]{2,1,0:T(8,128)(2,1)S(1)} %fusion.4), channel_id=1, source_target_pairs={{0,2},{1,3},{2,0},{3,1},{4,6},{5,7},{6,4},{7,5},{8,10},{9,11},{10,... | collective-permute-start | bytes 786440 | tf_op jit(solution)/shard_map/ppermute | solution.py:209
  7.5 1.6 %forward.3 = f32[2,64,8,256]{3,2,1,0:T(8,128)S(1)} custom-call(bf16[2,64,2,8,256]{4,3,2,1,0:T(8,128)(2,1)} %bitcast.31, s32[4,16]{1,0:T(4,128)} %bitcast.37, bf16[2,256,256]{2,1,0:T(8,128)(2,1)} %bitcast.34), custom_call_target="tpu_custom_call" | custom-call | flops 268435456 | bytes 2359552 | tf_op jit(solution)/shard_map/forward/pallas_call | solution.py:172
  9.1 0.7 %collective-permute-start.1 = (f16[64,8,256]{2,1,0:T(8,128)(2,1)S(1)}, f16[64,8,256]{2,1,0:T(8,128)(2,1)S(1)}, u32[]{:S(2)}, u32[]{:S(2)}) collective-permute-start(f16[64,8,256]{2,1,0:T(8,128)(2,1)S(1)} %fusion.6), channel_id=1, source_target_pairs={{0,1},{1,0},{2,3},{3,2},{4,5},{5,4},{6,7},{7,6},{8,9},{9,8},{10,11... | collective-permute-start | bytes 786440 | tf_op jit(solution)/shard_map/ppermute | solution.py:209
  9.9 5.4 %collective-permute-done.2 = f16[64,8,256]{2,1,0:T(8,128)(2,1)S(1)} collective-permute-done((f16[64,8,256]{2,1,0:T(8,128)(2,1)S(1)}, f16[64,8,256]{2,1,0:T(8,128)(2,1)S(1)}, u32[]{:S(2)}, u32[]{:S(2)}) %collective-permute-start.2) | collective-permute-done | bytes 262176 | tf_op jit(solution)/shard_map/ppermute | solution.py:209
  15.3 0.1 fusion.2
  15.4 20.7 %all_to_all.10 = f16[64,8,256]{2,1,0:T(8,128)(2,1)S(1)} all-to-all(f16[64,8,256]{2,1,0:T(8,128)(2,1)S(1)} %fusion.2), channel_id=1, replica_groups=mesh['freq'=64,'panel'=4] {'freq'}, dimensions={0} | all-to-all | bytes 524288 | tf_op jit(solution)/shard_map/all_to_all | solution.py:217
  36.1 0.6 copy-done
  36.7 1.8 %window.1 = bf16[64,8,256]{2,1,0:T(8,128)(2,1)S(1)} custom-call(bf16[2,512,512]{2,1,0:T(8,128)(2,1)S(1)} %copy-done.1, f32[512,256]{1,0:T(8,128)S(1)} %bitcast_convert_fusion.traces_ref, s32[4,256]{1,0:T(4,128)S(1)} %copy-done), custom_call_target="tpu_custom_call" | custom-call | flops 805306368 | bytes 1839104 | tf_op jit(solution)/shard_map/window/pallas_call | solution.py:172
  38.5 17.2 %all_to_all.11.own_ref = bf16[64,8,256]{2,1,0:T(8,128)(2,1)S(1)} all-to-all(bf16[64,8,256]{2,1,0:T(8,128)(2,1)S(1)} %window.1), channel_id=1, replica_groups=mesh['freq'=64,'panel'=4] {'freq'}, dimensions={0} | all-to-all | bytes 524288 | tf_op jit(solution)/shard_map/all_to_all | solution.py:226
  55.7 3.6 %collective-permute-start.3 = (bf16[64,8,256]{2,1,0:T(8,128)(2,1)S(1)}, bf16[64,8,256]{2,1,0:T(8,128)(2,1)S(1)}, u32[]{:S(2)}, u32[]{:S(2)}) collective-permute-start(bf16[64,8,256]{2,1,0:T(8,128)(2,1)S(1)} %all_to_all.11.own_ref), channel_id=1, source_target_pairs={{0,1},{1,0},{2,3},{3,2},{4,5},{5,4},{6,7},{7,6},{8,9},{9,8},{10,11... | collective-permute-start | bytes 786440 | tf_op jit(solution)/shard_map/ppermute | solution.py:209
  59.4 2.7 %collective-permute-start.6 = (bf16[64,8,128]{2,1,0:T(8,128)(2,1)S(1)}, bf16[64,8,128]{2,1,0:T(8,128)(2,1)S(1)}, u32[]{:S(2)}, u32[]{:S(2)}) collective-permute-start(bf16[64,8,128]{2,1,0:T(8,128)(2,1)S(1)} %get-tuple-element.17), channel_id=1, source_target_pairs={{0,2},{1,3},{2,0},{3,1},{4,6},{5,7},{6,4},{7,5},{8,10},{9,11},{10,... | collective-permute-start | bytes 393224 | tf_op jit(solution)/shard_map/ppermute | solution.py:209
  62.1 0.3 collective-permute-start.4
  62.4 2.0 %near.1 = (f32[512,256]{1,0:T(8,128)S(1)}, bf16[256,1024]{1,0:T(8,128)(2,1)S(1)}) custom-call(bf16[2,64,2,8,256]{4,3,2,1,0:T(8,128)(2,1)} %bitcast.32, s32[4,16]{1,0:T(4,128)} %bitcast.38, bf16[64,8,256]{2,1,0:T(8,128)(2,1)S(1)} %all_to_all.11.own_ref, bf16[64,8,256]{2,1,0:T(8,128)(2,1)S(1)} %collective-permute-done.3.other_ref, f32[512,256]{1,0:T(8,128)} %bitcast.35), custom_call_target="tpu_custom_call" | custom-call | flops 268435456 | bytes 3145984 | tf_op jit(solution)/shard_map/near/pallas_call | solution.py:172
  64.4 1.6 %collective-permute-done.6.own_ref = bf16[64,8,128]{2,1,0:T(8,128)(2,1)S(1)} collective-permute-done((bf16[64,8,128]{2,1,0:T(8,128)(2,1)S(1)}, bf16[64,8,128]{2,1,0:T(8,128)(2,1)S(1)}, u32[]{:S(2)}, u32[]{:S(2)}) %collective-permute-start.6) | collective-permute-done | bytes 131104 | tf_op jit(solution)/shard_map/ppermute | solution.py:209
  66.0 1.0 %collective-permute-start.7 = (bf16[64,8,128]{2,1,0:T(8,128)(2,1)S(1)}, bf16[64,8,128]{2,1,0:T(8,128)(2,1)S(1)}, u32[]{:S(2)}, u32[]{:S(2)}) collective-permute-start(bf16[64,8,128]{2,1,0:T(8,128)(2,1)S(1)} %collective-permute-done.6.own_ref), channel_id=1, source_target_pairs={{0,1},{1,0},{2,3},{3,2},{4,5},{5,4},{6,7},{7,6},{8,9},{9,8},{10,11... | collective-permute-start | bytes 393224 | tf_op jit(solution)/shard_map/ppermute | solution.py:209
  67.0 1.7 %collective-permute-done.4.own_ref = bf16[64,8,128]{2,1,0:T(8,128)(2,1)S(1)} collective-permute-done((bf16[64,8,128]{2,1,0:T(8,128)(2,1)S(1)}, bf16[64,8,128]{2,1,0:T(8,128)(2,1)S(1)}, u32[]{:S(2)}, u32[]{:S(2)}) %collective-permute-start.4) | collective-permute-done | bytes 131104 | tf_op jit(solution)/shard_map/ppermute | solution.py:209
  68.7 1.0 %collective-permute-start.5 = (bf16[64,8,128]{2,1,0:T(8,128)(2,1)S(1)}, bf16[64,8,128]{2,1,0:T(8,128)(2,1)S(1)}, u32[]{:S(2)}, u32[]{:S(2)}) collective-permute-start(bf16[64,8,128]{2,1,0:T(8,128)(2,1)S(1)} %collective-permute-done.4.own_ref), channel_id=1, source_target_pairs={{0,1},{1,0},{2,3},{3,2},{4,5},{5,4},{6,7},{7,6},{8,9},{9,8},{10,11... | collective-permute-start | bytes 393224 | tf_op jit(solution)/shard_map/ppermute | solution.py:209
  69.7 0.3 middle.1.done_ref
  70.0 0.6 collective-permute-done.5.other_ref
  70.7 1.1 %last.1 = f32[512,256]{1,0:T(8,128)} custom-call(bf16[256,1024]{1,0:T(8,128)(2,1)S(1)} %get-tuple-element.13.far_ref, bf16[64,8,128]{2,1,0:T(8,128)(2,1)S(1)} %collective-permute-done.4.own_ref, bf16[64,8,128]{2,1,0:T(8,128)(2,1)S(1)} %collective-permute-done.5.other_ref, f32[512,256]{1,0:T(8,128)S(1)} %get-tuple-element.15.base_ref, ...), custom_call_target="tpu_custom_call" | custom-call | flops 134217728 | bytes 2097152 | tf_op jit(solution)/shard_map/last/pallas_call | solution.py:172
  (10 shorter events, 0.2 us)
Async XLA Ops:
  1.6 4.4 %collective-permute-start = (f16[64,8,256]{2,1,0:T(8,128)(2,1)S(1)}, f16[64,8,256]{2,1,0:T(8,128)(2,1)S(1)}, u32[]{:S(2)}, u32[]{:S(2)}) collective-permute-start(f16[64,8,256]{2,1,0:T(8,128)(2,1)S(1)} %fusion.5), channel_id=1, source_target_pairs={{0,1},{1,0},{2,3},{3,2},{4,5},{5,4},{6,7},{7,6},{8,9},{9,8},{10,11... | collective-permute-start | bytes 786440 | tf_op jit(solution)/shard_map/ppermute | solution.py:209
  6.2 9.1 %collective-permute-start.2 = (f16[64,8,256]{2,1,0:T(8,128)(2,1)S(1)}, f16[64,8,256]{2,1,0:T(8,128)(2,1)S(1)}, u32[]{:S(2)}, u32[]{:S(2)}) collective-permute-start(f16[64,8,256]{2,1,0:T(8,128)(2,1)S(1)} %fusion.4), channel_id=1, source_target_pairs={{0,2},{1,3},{2,0},{3,1},{4,6},{5,7},{6,4},{7,5},{8,10},{9,11},{10,... | collective-permute-start | bytes 786440 | tf_op jit(solution)/shard_map/ppermute | solution.py:209
  9.1 27.0 %copy-start.1 = (bf16[2,512,512]{2,1,0:T(8,128)(2,1)S(1)}, bf16[2,512,512]{2,1,0:T(8,128)(2,1)}, u32[]{:S(2)}) copy-start(bf16[2,512,512]{2,1,0:T(8,128)(2,1)} %constant.2.clone.pair_ref) | copy-start | bytes 3145732
  9.1 6.1 %collective-permute-start.1 = (f16[64,8,256]{2,1,0:T(8,128)(2,1)S(1)}, f16[64,8,256]{2,1,0:T(8,128)(2,1)S(1)}, u32[]{:S(2)}, u32[]{:S(2)}) collective-permute-start(f16[64,8,256]{2,1,0:T(8,128)(2,1)S(1)} %fusion.6), channel_id=1, source_target_pairs={{0,1},{1,0},{2,3},{3,2},{4,5},{5,4},{6,7},{7,6},{8,9},{9,8},{10,11... | collective-permute-start | bytes 786440 | tf_op jit(solution)/shard_map/ppermute | solution.py:209
  36.0 0.7 copy-start
  55.7 6.7 %collective-permute-start.3 = (bf16[64,8,256]{2,1,0:T(8,128)(2,1)S(1)}, bf16[64,8,256]{2,1,0:T(8,128)(2,1)S(1)}, u32[]{:S(2)}, u32[]{:S(2)}) collective-permute-start(bf16[64,8,256]{2,1,0:T(8,128)(2,1)S(1)} %all_to_all.11.own_ref), channel_id=1, source_target_pairs={{0,1},{1,0},{2,3},{3,2},{4,5},{5,4},{6,7},{7,6},{8,9},{9,8},{10,11... | collective-permute-start | bytes 786440 | tf_op jit(solution)/shard_map/ppermute | solution.py:209
  59.4 6.6 %collective-permute-start.6 = (bf16[64,8,128]{2,1,0:T(8,128)(2,1)S(1)}, bf16[64,8,128]{2,1,0:T(8,128)(2,1)S(1)}, u32[]{:S(2)}, u32[]{:S(2)}) collective-permute-start(bf16[64,8,128]{2,1,0:T(8,128)(2,1)S(1)} %get-tuple-element.17), channel_id=1, source_target_pairs={{0,2},{1,3},{2,0},{3,1},{4,6},{5,7},{6,4},{7,5},{8,10},{9,11},{10,... | collective-permute-start | bytes 393224 | tf_op jit(solution)/shard_map/ppermute | solution.py:209
  62.1 6.6 %collective-permute-start.4 = (bf16[64,8,128]{2,1,0:T(8,128)(2,1)S(1)}, bf16[64,8,128]{2,1,0:T(8,128)(2,1)S(1)}, u32[]{:S(2)}, u32[]{:S(2)}) collective-permute-start(bf16[64,8,128]{2,1,0:T(8,128)(2,1)S(1)} %get-tuple-element.18), channel_id=1, source_target_pairs={{0,2},{1,3},{2,0},{3,1},{4,6},{5,7},{6,4},{7,5},{8,10},{9,11},{10,... | collective-permute-start | bytes 393224 | tf_op jit(solution)/shard_map/ppermute | solution.py:209
  66.0 3.7 %collective-permute-start.7 = (bf16[64,8,128]{2,1,0:T(8,128)(2,1)S(1)}, bf16[64,8,128]{2,1,0:T(8,128)(2,1)S(1)}, u32[]{:S(2)}, u32[]{:S(2)}) collective-permute-start(bf16[64,8,128]{2,1,0:T(8,128)(2,1)S(1)} %collective-permute-done.6.own_ref), channel_id=1, source_target_pairs={{0,1},{1,0},{2,3},{3,2},{4,5},{5,4},{6,7},{7,6},{8,9},{9,8},{10,11... | collective-permute-start | bytes 393224 | tf_op jit(solution)/shard_map/ppermute | solution.py:209
  68.7 1.9 %collective-permute-start.5 = (bf16[64,8,128]{2,1,0:T(8,128)(2,1)S(1)}, bf16[64,8,128]{2,1,0:T(8,128)(2,1)S(1)}, u32[]{:S(2)}, u32[]{:S(2)}) collective-permute-start(bf16[64,8,128]{2,1,0:T(8,128)(2,1)S(1)} %collective-permute-done.4.own_ref), channel_id=1, source_target_pairs={{0,1},{1,0},{2,3},{3,2},{4,5},{5,4},{6,7},{7,6},{8,9},{9,8},{10,11... | collective-permute-start | bytes 393224 | tf_op jit(solution)/shard_map/ppermute | solution.py:209
